TPU v7x, 512 devices: a whole 4x8x8 slice. The times are simulated.
512 devices in a mesh: exp: 32 (over x_lo, z, core), ccd: 16 (over x_hi, y).
Axes of the slice: x: 4 (x_hi: 2, x_lo: 2; x = x_hi * 2 + x_lo), y: 8, z: 8, core: 2. Of those that a mesh axis runs over, the one named last changes fastest.
Arguments:
- pixels: bfloat16 [32, 16000, 4, 128], P('exp', 'ccd'), may hold values from -24 to 24
- psf_proj: bfloat16 [32, 100, 2160], P('ccd'), may hold values from -0.5 to 0.5
- resolution: float32 [800, 11, 512], P('ccd', None, 'exp'), may hold values from 0.02 to 0.16
- basis: float32 [10, 528], replicated, may hold values from -4 to 4
- sky_fibres: int32 [96], replicated, may hold values from 0 to 799, as said below
- fibre_slot: int32 [800], P('ccd'), may hold values from 0 to 799, as said below
- band_shift: int32 [800], P('ccd'), may hold values from -3 to 3
Outputs:
- sky_subtracted: float32 [32, 800, 512], P(None, 'ccd', 'exp')
- noise_rms: float32 [800, 512], P('ccd', 'exp')
Inputs may be any that keep to these rules, and one draw needn't show every extreme that they name: `sky_fibres`: 96 distinct fibre numbers, listed group by group: entries g * 6 to (g + 1) * 6 - 1 are fibres of the group g of 50 consecutive fibres. `fibre_slot`: for each group g of 50 consecutive fibres, a permutation of the slots g * 50 to (g + 1) * 50 - 1.
All inputs are finite; a program needn't handle non-finite values.
Results may differ from a plain program's by a relative error of at most 0.00095.
Values may be sent and summed in bfloat16 or wider, within the bound.
No kernel may reach another device: no remote copies, remote signals or barrier semaphores. Data moves between devices by JAX's collectives and lax.ppermute only.
A program may use at most 64 MiB of HBM per device.

v0:
```python
import jax
import jax.numpy as jnp
from jax import lax
from jax.sharding import PartitionSpec as P

BPIX = 500
MARG = 20
ROWS = 4
BAND = 11
SHIFT = 3
FC = 50
SPAN = 540
highest = lax.Precision.HIGHEST


def extended(x, sides, width):
    for axis, dim in sides:
        size, length = (lax.axis_size(axis), x.shape[dim])
        up = [(i, (i + 1) % size) for i in range(size - 1)]
        down = [(j, i) for i, j in up]
        last = lax.slice_in_dim(x, length - width, length, axis=dim)
        leading = lax.slice_in_dim(x, 0, width, axis=dim)
        before = lax.ppermute(last, axis, up)
        after = lax.ppermute(leading, axis, down)
        x = jnp.concatenate([before, x, after], axis=dim)
    return x


def band_model(pieces, spectra, shifts):
    length = pieces.shape[2]

    def window_of(shift):
        return lax.dynamic_slice(
            spectra, (jnp.int32(0), shift + SHIFT), (spectra.shape[0], length + BAND - 1)
        )

    windows = jax.vmap(window_of)(shifts)
    total = jnp.zeros((pieces.shape[0], spectra.shape[0], length), jnp.float32)
    for offset in range(BAND):
        total = total + pieces[:, offset, None, :] * windows[:, :, offset : offset + length]
    return total


def solve_small(gram, target):
    factor = jnp.linalg.cholesky(gram)
    return jax.scipy.linalg.cho_solve((factor, True), target[..., None])[..., 0]


def shards(pixels, psf_proj, resolution, basis, sky_fibres, fibre_slot, band_shift):
    padded = extended(pixels, (("ccd", 1),), MARG)
    pixvar = (0.25 + jnp.square(padded.astype(jnp.float32))).astype(jnp.bfloat16)
    proj_square = jnp.square(psf_proj.astype(jnp.float32)).astype(jnp.bfloat16)
    groups = pixels.shape[3]
    flux_parts = []
    var_parts = []
    for block in range(psf_proj.shape[0]):
        lower = block * BPIX
        window = padded[0, lower : lower + SPAN].reshape(SPAN * ROWS, groups)
        window_var = pixvar[0, lower : lower + SPAN].reshape(SPAN * ROWS, groups)
        flux_parts.append(jnp.dot(psf_proj[block], window, preferred_element_type=jnp.float32))
        var_parts.append(
            jnp.dot(proj_square[block], window_var, preferred_element_type=jnp.float32)
        )
    flux_slots = jnp.concatenate(flux_parts, 0).reshape(FC, ROWS * groups)
    var_slots = jnp.concatenate(var_parts, 0).reshape(FC, ROWS * groups)
    group_base = lax.axis_index("ccd") * FC
    local_slot = fibre_slot - group_base
    flux_rows = jnp.take(flux_slots, local_slot, axis=0)
    var_rows = jnp.take(var_slots, local_slot, axis=0)
    fibre_ids = group_base + jnp.arange(FC, dtype=jnp.int32)
    skymask = jnp.any(fibre_ids[:, None] == sky_fibres[None, :], axis=1).astype(jnp.float32)
    model = band_model(
        lax.all_gather(resolution.astype(jnp.bfloat16), "exp", axis=2, tiled=True).astype(
            jnp.float32
        ),
        basis,
        band_shift,
    )
    weight = skymask[:, None] / var_rows
    weighted = model * weight[:, None, :]
    gram = jnp.einsum("fkw,flw->kl", weighted, model, precision=highest)
    target = jnp.einsum("fkw,fw->k", weighted, flux_rows, precision=highest)
    gram, target = lax.psum((gram, target), "ccd")
    coeffs = solve_small(gram, target)
    residual = flux_rows - jnp.einsum("k,fkw->fw", coeffs, model, precision=highest)
    sky_subtracted = lax.all_to_all(residual[None], "exp", split_axis=2, concat_axis=0, tiled=True)
    centred = sky_subtracted - jnp.mean(sky_subtracted, axis=0)
    noise_rms = jnp.sqrt(jnp.mean(jnp.square(centred), axis=0) + 1e-06)
    return (sky_subtracted, noise_rms)


def solution(mesh):
    in_specs = (
        P("exp", "ccd", None, None),
        P("ccd", None, None),
        P("ccd", None, "exp"),
        P(),
        P(),
        P("ccd"),
        P("ccd"),
    )
    out_specs = (P(None, "ccd", "exp"), P("ccd", "exp"))
    return jax.shard_map(shards, mesh=mesh, in_specs=in_specs, out_specs=out_specs, check_vma=False)
```

profile of v0, /device:TPU:1, one launch (start us, length us, event | category | flops | bytes accessed | tf_op | source)
XLA Modules:
  0.0 216.6 jit_solution(9551410797200062274)
XLA Ops:
  0.6 1.4 fusion.23
  2.0 4.0 %collective-permute-start = (bf16[1,20,4,128]{3,2,1,0:T(4,128)(2,1)}, bf16[1,20,4,128]{3,2,1,0:T(4,128)(2,1)S(1)}, u32[]{:S(2)}, u32[]{:S(2)}) collective-permute-start(bf16[1,20,4,128]{3,2,1,0:T(4,128)(2,1)} %get-tuple-element.38), channel_id=1, source_target_pairs={{0,1},{1,2},{2,3},{3,4},{4,5},{5,6},{6,7},{7,8},{8,9},{9,10},{10,1... | collective-permute-start | bytes 61448 | tf_op jit(solution)/shard_map/ppermute | solution.py:23
  6.0 1.3 collective-permute-start.1
  7.4 0.9 convert_element_type.41
  8.3 45.0 %all_gather.3 = bf16[50,11,512]{0,2,1:T(8,128)(2,1)S(1)} all-gather(bf16[50,11,16]{0,2,1:T(8,128)(2,1)S(1)} %convert_element_type.41), channel_id=1, replica_groups=mesh['exp'=32,'ccd'=16] {'exp'}, dimensions={2}, use_global_device_ids=true | all-gather | bytes 580800 | tf_op jit(solution)/shard_map/all_gather | solution.py:73
  53.5 1.2 slice_bitcast_fusion.18
  54.7 1.1 copy.62
  55.8 1.7 copy.63
  57.5 1.7 copy.64
  59.2 1.7 copy.65
  60.9 1.7 copy.66
  62.6 1.7 copy.67
  68.9 61.5 %while.1 = (s32[]{:T(128)}, f32[10,528]{1,0:T(8,128)S(1)}, s32[50,2]{0,1:T(2,128)S(1)}, f32[50,10,522]{2,1,0:T(8,128)S(1)}, s32[]{:T(128)}) while((s32[]{:T(128)}, f32[10,528]{1,0:T(8,128)S(1)}, s32[50,2]{0,1:T(2,128)S(1)}, f32[50,10,522]{2,1,0:T(8,128)S(1)}, s32[]{:T(128)}) %tuple.39), condition=%wide.while_cond, body=%wide.while_body.sunk | while | flops 2 | bytes 82017 | solution.py:33
  130.5 1.4 multiply_convert_fusion
  132.2 6.5 %multiply_add_fusion = f32[50,10,512]{2,1,0:T(8,128)} fusion(f32[50,10,522]{2,1,0:T(8,128)S(1)} %get-tuple-element.10, f32[50,512]{1,0:T(8,128)S(1)} %copy-done.10, f32[50,512]{1,0:T(8,128)S(1)} %copy-done.9, f32[50,512]{1,0:T(8,128)S(1)} %copy-done.8, f32[50,512]{1,0:T(8,128)} %copy.69, f32[50,512]{1,0:T(8,128)} %copy.68, f32[50,512]{1,0:T(8,128)} %copy.67, ...), kind=kLoop, calls=%fused_computation.10 | loop fusion | flops 5376000 | bytes 13414400 | tf_op jit(solution)/shard_map/add | solution.py:40
  138.8 1.1 copy-done.1
  141.2 3.7 %add_convert_fusion = bf16[1,1040,4,128]{3,2,1,0:T(4,128)(2,1)S(1)} fusion(bf16[1,20,4,128]{3,2,1,0:T(4,128)(2,1)S(1)} %collective-permute-done.1, bf16[1,1000,4,128]{3,2,1,0:T(4,128)(2,1)S(1)} %copy-done.1, bf16[1,20,4,128]{3,2,1,0:T(4,128)(2,1)S(1)} %collective-permute-done), kind=kLoop, calls=%fused_computation.8 | loop fusion | flops 3194880 | bytes 2129920 | tf_op jit(solution)/shard_map/convert_element_type | solution.py:51
  147.4 2.3 %fusion.4 = f32[10,10]{0,1:T(8,128)S(1)} fusion(f32[50,10,512]{2,1,0:T(8,128)S(1)} %copy-done, f32[50,512]{1,0:T(8,128)S(1)} %get-tuple-element.41), kind=kOutput, calls=%fused_computation.13 | convolution fusion | flops 30976000 | bytes 1126800 | tf_op jit(solution)/shard_map/fkw,flw->kl/dot_general | solution.py:81
  149.7 2.0 fusion.7
  151.7 37.4 %all-reduce.1 = (f32[10,10]{0,1:T(8,128)S(1)}, f32[10]{0:T(128)S(1)}) all-reduce(f32[10,10]{0,1:T(8,128)S(1)} %fusion.4, f32[10]{0:T(128)S(1)} %fusion.7), channel_id=1, replica_groups=mesh['exp'=32,'ccd'=16] {'ccd'}, use_global_device_ids=true, to_apply=%region_1.3 | all-reduce | flops 110 | bytes 880 | tf_op jit(solution)/shard_map/psum | solution.py:83
  192.6 0.9 fusion.24
  194.2 1.3 reduce.7
  195.8 18.6 %all_to_all.18 = f32[32,1,800]{2,1,0:T(1,128)S(1)} all-to-all(f32[32,1,800]{2,1,0:T(1,128)S(1)} %reshape.151), channel_id=1, replica_groups=mesh['exp'=32,'ccd'=16] {'exp'}, dimensions={0} | all-to-all | bytes 204800 | tf_op jit(solution)/shard_map/all_to_all | solution.py:86
  214.4 0.9 reduce.8
  (223 shorter events, 75.8 us)
Async XLA Ops:
  2.0 136.8 %collective-permute-start = (bf16[1,20,4,128]{3,2,1,0:T(4,128)(2,1)}, bf16[1,20,4,128]{3,2,1,0:T(4,128)(2,1)S(1)}, u32[]{:S(2)}, u32[]{:S(2)}) collective-permute-start(bf16[1,20,4,128]{3,2,1,0:T(4,128)(2,1)} %get-tuple-element.38), channel_id=1, source_target_pairs={{0,1},{1,2},{2,3},{3,4},{4,5},{5,6},{6,7},{7,8},{8,9},{9,10},{10,1... | collective-permute-start | bytes 61448 | tf_op jit(solution)/shard_map/ppermute | solution.py:23
  6.0 132.7 %collective-permute-start.1 = (bf16[1,20,4,128]{3,2,1,0:T(4,128)(2,1)}, bf16[1,20,4,128]{3,2,1,0:T(4,128)(2,1)S(1)}, u32[]{:S(2)}, u32[]{:S(2)}) collective-permute-start(bf16[1,20,4,128]{3,2,1,0:T(4,128)(2,1)} %get-tuple-element.39), channel_id=1, source_target_pairs={{1,0},{2,1},{3,2},{4,3},{5,4},{6,5},{7,6},{8,7},{9,8},{10,9},{11,1... | collective-permute-start | bytes 61448 | tf_op jit(solution)/shard_map/ppermute | solution.py:24
  57.5 11.5 %copy-start.4 = (f32[10,528]{1,0:T(8,128)S(1)}, f32[10,528]{1,0:T(8,128)}, u32[]{:S(2)}) copy-start(f32[10,528]{1,0:T(8,128)} %param.12) | copy-start | bytes 63364
  65.2 65.3 %copy-start.11 = (s32[50]{0:T(128)S(1)}, s32[50]{0:T(128)}, u32[]{:S(2)}) copy-start(s32[50]{0:T(128)} %param.14) | copy-start | bytes 604
  66.7 65.2 %copy-start.12 = (s32[96]{0:T(128)S(1)}, s32[96]{0:T(128)}, u32[]{:S(2)}) copy-start(s32[96]{0:T(128)} %param.13) | copy-start | bytes 1156
  66.7 65.4 %copy-start.5 = (f32[50,512]{1,0:T(8,128)S(1)}, f32[50,512]{1,0:T(8,128)}, u32[]{:S(2)}) copy-start(f32[50,512]{1,0:T(8,128)} %copy.63) | copy-start | bytes 307204
  66.7 65.4 %copy-start.6 = (f32[50,512]{1,0:T(8,128)S(1)}, f32[50,512]{1,0:T(8,128)}, u32[]{:S(2)}) copy-start(f32[50,512]{1,0:T(8,128)} %copy.64) | copy-start | bytes 307204
  66.7 65.4 %copy-start.7 = (f32[50,512]{1,0:T(8,128)S(1)}, f32[50,512]{1,0:T(8,128)}, u32[]{:S(2)}) copy-start(f32[50,512]{1,0:T(8,128)} %copy.65) | copy-start | bytes 307204
  130.5 1.7 copy-start.8
  130.5 1.7 copy-start.9
  130.5 1.7 copy-start.10
  132.2 6.5 %copy-start.2 = (bf16[2,100,2160]{2,0,1:T(2,128)(2,1)S(1)}, bf16[2,100,2160]{2,0,1:T(2,128)(2,1)}, u32[]{:S(2)}) copy-start(bf16[2,100,2160]{2,0,1:T(2,128)(2,1)} %param.10) | copy-start | bytes 2592004
  138.6 1.2 copy-start.1
  145.9 1.4 copy-start
  215.9 0.7 copy-start.3
where the time goes:
time: 220 us; the launch traced here: 217 us
  blocking collectives  101 us (46%)
  local copies, waits for them, and re-layouts  82 us (37%)
  other arithmetic  20.4 us (9%)
  matrix products  6.68 us (3%)
  starting transfers between devices  5.31 us (2%)
    gather x150, local copies, waits for them, and re-layouts  61.4 us
    all_gather x1, blocking collectives, shards(): lax.all_gather(resolution.astype(jnp.bfloat16), 'exp', axis=2, tiled=True)  45 us
    psum x1, blocking collectives, shards(): gram, target = lax.psum((gram, target), 'ccd')  37.4 us
    all_to_all x1, blocking collectives, shards(): lax.all_to_all(residual[None], 'exp', split_axis=2, concat_axis=0, tiled=...  18.6 us
    mul x12, local copies, waits for them, and re-layouts, band_model(): pieces[:, offset, None, :] * windows[:, :, offset:offset + length]  14.7 us
    add x1, other arithmetic, band_model(): total + pieces[:, offset, None, :] * windows[:, :, offset:offset + length]  6.47 us
  transfers between devices with their start and end apart: 2, of which 0 were waited for; matrix products, arithmetic and copies ran while one was open for 40% of the time, Pallas kernels for 0%

commit v1 on v0

--- a/solution.py
+++ b/solution.py
@@ -11,6 +11,19 @@
 FC = 50
 SPAN = 540
 highest = lax.Precision.HIGHEST
+
+
+def _return_all_weights(state):
+    upper = jnp.concatenate(
+        jax.lax.all_to_all(
+            jnp.stack([state] * jax.lax.axis_size("exp")),
+            axis_name="exp",
+            split_axis=0,
+            concat_axis=0,
+        ),
+        axis=2,
+    )
+    return upper
 
 
 def extended(x, sides, width):
@@ -70,11 +83,7 @@
     fibre_ids = group_base + jnp.arange(FC, dtype=jnp.int32)
     skymask = jnp.any(fibre_ids[:, None] == sky_fibres[None, :], axis=1).astype(jnp.float32)
     model = band_model(
-        lax.all_gather(resolution.astype(jnp.bfloat16), "exp", axis=2, tiled=True).astype(
-            jnp.float32
-        ),
-        basis,
-        band_shift,
+        _return_all_weights(resolution.astype(jnp.bfloat16)).astype(jnp.float32), basis, band_shift
     )
     weight = skymask[:, None] / var_rows
     weighted = model * weight[:, None, :]

time: 220 us -> 199 us (0.905); the launches traced: 217 us -> 198 us
  blocking collectives: 101 us -> 60.8 us
  starting transfers between devices: 5.31 us -> 17.8 us
  local copies, waits for them, and re-layouts: 82 us -> 89.4 us
    all_gather x1 -> x0, blocking collectives: 45 us -> none  [shards(): lax.all_gather(resolution.astype(jnp.bfloat16), 'exp', axis=2, tiled=True)]
    all_to_all x0 -> x1, starting transfers between devices: none -> 13.1 us  [_return_all_weights(): jax.lax.all_to_all(jnp.stack([state] * jax.lax.axis_size('exp')), axis_na...]
    unnamed x30 -> x33, local copies, waits for them, and re-layouts: 2.53 us -> 9.32 us
    all_to_all x1, blocking collectives: 18.6 us -> 24 us  [shards(): lax.all_to_all(residual[None], 'exp', split_axis=2, concat_axis=0, tiled=...]
    gather x150, local copies, waits for them, and re-layouts: 61.4 us -> 65.8 us
    mul x12, local copies, waits for them, and re-layouts: 14.7 us -> 12.1 us  [band_model(): pieces[:, offset, None, :] * windows[:, :, offset:offset + length]]
  transfers between devices with their start and end apart: 2 -> 3, of which waited for: 0 -> 0; matrix products, arithmetic and copies ran while one was open for 40% -> 39% of each run, Pallas kernels for 0% -> 0%
where the time goes in v1:
time: 199 us; the launch traced here: 198 us
  local copies, waits for them, and re-layouts  89.4 us (45%)
  blocking collectives  60.8 us (31%)
  other arithmetic  20.7 us (10%)
  starting transfers between devices  17.8 us (9%)
  matrix products  8.08 us (4%)
    gather x150, local copies, waits for them, and re-layouts  65.8 us
    psum x1, blocking collectives, shards(): gram, target = lax.psum((gram, target), 'ccd')  36.8 us
    all_to_all x1, blocking collectives, shards(): lax.all_to_all(residual[None], 'exp', split_axis=2, concat_axis=0, tiled=...  24 us
    all_to_all x1, starting transfers between devices, _return_all_weights(): jax.lax.all_to_all(jnp.stack([state] * jax.lax.axis_size('exp')), axis_na...  13.1 us
    mul x12, local copies, waits for them, and re-layouts, band_model(): pieces[:, offset, None, :] * windows[:, :, offset:offset + length]  12.1 us
    unnamed x33, local copies, waits for them, and re-layouts  9.32 us
    add x1, other arithmetic, band_model(): total + pieces[:, offset, None, :] * windows[:, :, offset:offset + length]  5.82 us
  transfers between devices with their start and end apart: 3, of which 0 were waited for; matrix products, arithmetic and copies ran while one was open for 39% of the time, Pallas kernels for 0%

profile of v1, /device:TPU:1, one launch (start us, length us, event | category | flops | bytes accessed | tf_op | source)
XLA Modules:
  0.0 198.0 jit_solution(3949466347977027966)
XLA Ops:
  0.6 0.9 convert_element_type.47
  1.8 3.2 %reshape.158 = bf16[32,2,4400]{2,1,0:T(2,128)(2,1)} reshape(bf16[32,11,16,50]{3,2,1,0:T(8,128)(2,1)S(1)} %broadcast_bitcast_fusion) | data formatting | bytes 1126400
  5.0 13.1 %all-to-all-start = ((bf16[32,2,4400]{2,1,0:T(2,128)(2,1)}), bf16[32,2,4400]{2,1,0:T(2,128)(2,1)}, u32[]{:S(2)}, u32[]{:S(2)}) async-start(bf16[32,2,4400]{2,1,0:T(2,128)(2,1)} %reshape.158), calls=%async_computation | async-start | bytes 1146880 | tf_op jit(solution)/shard_map/all_to_all | solution.py:18
  18.1 3.2 %collective-permute-start = (bf16[1,20,4,128]{3,2,1,0:T(4,128)(2,1)S(1)}, bf16[1,20,4,128]{3,2,1,0:T(4,128)(2,1)S(1)}, u32[]{:S(2)}, u32[]{:S(2)}) collective-permute-start(bf16[1,20,4,128]{3,2,1,0:T(4,128)(2,1)S(1)} %get-tuple-element.38), channel_id=1, source_target_pairs={{0,1},{1,2},{2,3},{3,4},{4,5},{5,6},{6,7},{7,8},{8,9},{9,10},{10,1... | collective-permute-start | bytes 61448 | tf_op jit(solution)/shard_map/ppermute | solution.py:36
  21.3 1.5 collective-permute-start.1
  22.9 65.9 %while.1 = (s32[]{:T(128)}, f32[10,528]{1,0:T(8,128)S(1)}, s32[50,2]{0,1:T(2,128)S(1)}, f32[50,10,522]{2,1,0:T(8,128)S(1)}, s32[]{:T(128)}) while((s32[]{:T(128)}, f32[10,528]{1,0:T(8,128)S(1)}, s32[50,2]{0,1:T(2,128)S(1)}, f32[50,10,522]{2,1,0:T(8,128)S(1)}, s32[]{:T(128)}) %tuple.39), condition=%wide.while_cond, body=%wide.while_body.sunk | while | flops 2 | bytes 82017 | solution.py:46
  88.7 2.3 %multiply_convert_fusion = bf16[2,100,2160]{2,1,0:T(8,128)(2,1)} fusion(bf16[2,100,2160]{2,0,1:T(2,128)(2,1)} %param.10), kind=kLoop, calls=%fused_computation.10 | loop fusion | flops 1296000 | bytes 1728000 | tf_op jit(solution)/shard_map/convert_element_type | solution.py:65
  92.8 3.7 %add_convert_fusion = bf16[1,1040,4,128]{3,2,1,0:T(4,128)(2,1)S(1)} fusion(bf16[1,20,4,128]{3,2,1,0:T(4,128)(2,1)S(1)} %collective-permute-done.1, bf16[1,1000,4,128]{3,2,1,0:T(4,128)(2,1)S(1)} %copy-done.1, bf16[1,20,4,128]{3,2,1,0:T(4,128)(2,1)S(1)} %collective-permute-done), kind=kLoop, calls=%fused_computation.9 | loop fusion | flops 3194880 | bytes 2129920 | tf_op jit(solution)/shard_map/convert_element_type | solution.py:64
  100.4 3.7 %reshape.159 = bf16[32,11,16,50]{3,2,1,0:T(8,128)(2,1)S(1)} reshape(bf16[32,2,4400]{2,1,0:T(2,128)(2,1)} %all-to-all-done) | data formatting | bytes 1126400
  104.5 1.2 slice_bitcast_fusion.18
  105.7 1.1 copy.54
  106.8 1.7 copy.55
  108.5 1.7 copy.56
  110.2 1.7 copy.57
  112.0 1.7 copy.58
  113.7 1.7 copy.59
  116.7 5.8 %multiply_add_fusion = f32[50,10,512]{2,1,0:T(8,128)S(1)} fusion(f32[50,10,522]{2,1,0:T(8,128)S(1)} %get-tuple-element.10, f32[50,512]{1,0:T(8,128)S(1)} %copy.64, f32[50,512]{1,0:T(8,128)S(1)} %copy.63, f32[50,512]{1,0:T(8,128)S(1)} %copy.62, f32[50,512]{1,0:T(8,128)S(1)} %copy.61, f32[50,512]{1,0:T(8,128)} %copy.60, f32[50,512]{1,0:T(8,128)} %copy.59, ...), kind=kLoop, calls=%fused_computation.11 | loop fusion | flops 5376000 | bytes 13414400 | tf_op jit(solution)/shard_map/add | solution.py:53
  122.6 2.3 %fusion.4 = f32[10,10]{0,1:T(8,128)S(1)} fusion(f32[50,10,512]{2,1,0:T(8,128)S(1)} %multiply_add_fusion, f32[50,512]{1,0:T(8,128)S(1)} %copy-done.7), kind=kOutput, calls=%fused_computation.14 | convolution fusion | flops 30976000 | bytes 1126800 | tf_op jit(solution)/shard_map/fkw,flw->kl/dot_general | solution.py:90
  124.9 2.0 %fusion.7 = f32[10]{0:T(128)S(1)} fusion(f32[50,10,512]{2,1,0:T(8,128)S(1)} %multiply_add_fusion, f32[50,512]{1,0:T(8,128)S(1)} %copy-done.7, f32[50,512,1]{1,0,2:T(8,128)S(1)} %copy-done.9), kind=kOutput, calls=%fused_computation.15 | convolution fusion | flops 3328000 | bytes 1228840 | tf_op jit(solution)/shard_map/fkw,fw->k/dot_general | solution.py:91
  126.9 36.8 %all-reduce.1 = (f32[10,10]{0,1:T(8,128)S(1)}, f32[10]{0:T(128)S(1)}) all-reduce(f32[10,10]{0,1:T(8,128)S(1)} %fusion.4, f32[10]{0:T(128)S(1)} %fusion.7), channel_id=1, replica_groups=mesh['exp'=32,'ccd'=16] {'ccd'}, use_global_device_ids=true, to_apply=%region_1.3 | all-reduce | flops 110 | bytes 880 | tf_op jit(solution)/shard_map/psum | solution.py:92
  167.1 2.3 %fusion.24 = f32[1,50,512]{2,0,1:T(1,128)S(1)} fusion(f32[10,1,1]{0,1,2:T(1,128)S(1)} %convolution_bitcast_fusion.2, f32[50,10,512]{2,1,0:T(8,128)} %copy-done), kind=kOutput, calls=%fused_computation.70 | convolution fusion | flops 3072000 | bytes 1126440 | tf_op jit(solution)/shard_map/k,fkw->fw/dot_general | solution.py:94
  170.2 1.3 reduce.7
  171.8 24.0 %all_to_all.23 = f32[32,1,800]{2,1,0:T(1,128)S(1)} all-to-all(f32[32,1,800]{2,1,0:T(1,128)S(1)} %reshape.160), channel_id=1, replica_groups=mesh['exp'=32,'ccd'=16] {'exp'}, dimensions={0} | all-to-all | bytes 204800 | tf_op jit(solution)/shard_map/all_to_all | solution.py:95
  195.8 0.9 reduce.8
  (228 shorter events, 78.9 us)
Async XLA Ops:
  1.7 16.4 %copy-start.1 = (bf16[1,1000,4,128]{3,2,1,0:T(4,128)(2,1)S(1)}, bf16[1,1000,4,128]{3,2,1,0:T(4,128)(2,1)}, u32[]{:S(2)}) copy-start(bf16[1,1000,4,128]{3,2,1,0:T(4,128)(2,1)} %param.9) | copy-start | bytes 3072004
  1.7 21.1 %copy-start.11 = (s32[50]{0:T(128)S(1)}, s32[50]{0:T(128)}, u32[]{:S(2)}) copy-start(s32[50]{0:T(128)} %param.15) | copy-start | bytes 604
  1.7 21.1 %copy-start.8 = (f32[10,528]{1,0:T(8,128)S(1)}, f32[10,528]{1,0:T(8,128)}, u32[]{:S(2)}) copy-start(f32[10,528]{1,0:T(8,128)} %param.12) | copy-start | bytes 63364
  1.8 87.0 %copy-start.10 = (s32[50]{0:T(128)S(1)}, s32[50]{0:T(128)}, u32[]{:S(2)}) copy-start(s32[50]{0:T(128)} %param.14) | copy-start | bytes 604
  5.0 86.1 %copy-start.12 = (s32[96]{0:T(128)S(1)}, s32[96]{0:T(128)}, u32[]{:S(2)}) copy-start(s32[96]{0:T(128)} %param.13) | copy-start | bytes 1156
  5.0 95.4 %all-to-all-start = ((bf16[32,2,4400]{2,1,0:T(2,128)(2,1)}), bf16[32,2,4400]{2,1,0:T(2,128)(2,1)}, u32[]{:S(2)}, u32[]{:S(2)}) async-start(bf16[32,2,4400]{2,1,0:T(2,128)(2,1)} %reshape.158), calls=%async_computation | async-start | bytes 1146880 | tf_op jit(solution)/shard_map/all_to_all | solution.py:18
  18.1 73.3 %collective-permute-start = (bf16[1,20,4,128]{3,2,1,0:T(4,128)(2,1)S(1)}, bf16[1,20,4,128]{3,2,1,0:T(4,128)(2,1)S(1)}, u32[]{:S(2)}, u32[]{:S(2)}) collective-permute-start(bf16[1,20,4,128]{3,2,1,0:T(4,128)(2,1)S(1)} %get-tuple-element.38), channel_id=1, source_target_pairs={{0,1},{1,2},{2,3},{3,4},{4,5},{5,6},{6,7},{7,8},{8,9},{9,10},{10,1... | collective-permute-start | bytes 61448 | tf_op jit(solution)/shard_map/ppermute | solution.py:36
  21.3 70.1 %collective-permute-start.1 = (bf16[1,20,4,128]{3,2,1,0:T(4,128)(2,1)S(1)}, bf16[1,20,4,128]{3,2,1,0:T(4,128)(2,1)S(1)}, u32[]{:S(2)}, u32[]{:S(2)}) collective-permute-start(bf16[1,20,4,128]{3,2,1,0:T(4,128)(2,1)S(1)} %get-tuple-element.39), channel_id=1, source_target_pairs={{1,0},{2,1},{3,2},{4,3},{5,4},{6,5},{7,6},{8,7},{9,8},{10,9},{11,1... | collective-permute-start | bytes 61448 | tf_op jit(solution)/shard_map/ppermute | solution.py:37
  88.7 2.6 %copy-start.3 = (bf16[2,100,2160]{2,0,1:T(2,128)(2,1)S(1)}, bf16[2,100,2160]{2,0,1:T(2,128)(2,1)}, u32[]{:S(2)}) copy-start(bf16[2,100,2160]{2,0,1:T(2,128)(2,1)} %param.10) | copy-start | bytes 2592004
  96.5 1.2 copy-start.2
  98.9 1.4 copy-start.5
  116.7 5.8 %copy-start.7 = (f32[50,512]{1,0:T(8,128)S(1)}, f32[50,512]{1,0:T(8,128)}, u32[]{:S(2)}) copy-start(f32[50,512]{1,0:T(8,128)} %get-tuple-element.41) | copy-start | bytes 307204
  122.5 2.3 %copy-start = (f32[50,10,512]{2,1,0:T(8,128)}, f32[50,10,512]{2,1,0:T(8,128)S(1)}, u32[]{:S(2)}) copy-start(f32[50,10,512]{2,1,0:T(8,128)S(1)} %multiply_add_fusion) | copy-start | bytes 3072004
  122.5 2.3 %copy-start.9 = (f32[50,512,1]{1,0,2:T(8,128)S(1)}, f32[50,512,1]{1,0,2:T(8,128)}, u32[]{:S(2)}) copy-start(f32[50,512,1]{1,0,2:T(8,128)} %get-tuple-element.40) | copy-start | bytes 307204
  124.9 44.6 %copy-start.6 = (f32[50,512]{1,0:T(8,128)S(1)}, f32[50,512]{1,0:T(8,128)}, u32[]{:S(2)}) copy-start(f32[50,512]{1,0:T(8,128)} %copy-done.5) | copy-start | bytes 307204
  197.3 0.7 copy-start.4
